TPU v7x, 512 devices: a whole 4x4x16 slice. The times are simulated.
512 devices in a mesh: tile: 128 (over z, x, core), layer: 4 (over y).
Axes of the slice: x: 4, y: 4, z: 16, core: 2. Of those that a mesh axis runs over, the one named last changes fastest.
Arguments:
- head_start: float32 [8, 8192, 512], P('layer', 'tile'), may hold values from -2 to 0.5
- soil_class: int32 [8, 8192, 512], P('layer', 'tile'), may hold values from 0 to 11
- land_mask: int32 [8192, 512], P('tile'), may hold values 0 or 1
- ks_table: float32 [12], replicated, may hold values from 0.2 to 5
- alpha_table: float32 [12], replicated, may hold values from 0.5 to 2
- store_table: float32 [12], replicated, may hold values from 0.5 to 2
- section: float32 [2048, 128], P('tile'), may hold values from -6 to 6
- cross_owner: int32 [128, 256], P('tile'), may hold values from 0 to 127, as said below
- cross_local: int32 [128, 256], P('tile'), may hold values from 0 to 15
- node_cell: int32 [128, 256, 128], P('tile'), may hold values from -1 to 32767, as said below
- bed_cond: float32 [128, 256, 128], P('tile'), may hold values from 0.5 to 4
Outputs:
- head: float32 [8, 8192, 512], P('layer', 'tile')
- inflow: float32 [2048, 128], P('tile', 'layer')
Inputs may be any that keep to these rules, and one draw needn't show every extreme that they name: `cross_owner`: no strip's row names one owner in more than 2 slots, and in every row some owner is named in exactly 2 slots. `node_cell`: -1 marks a node outside the strip; other values index the strip's top-layer cells row-major over 64 x 512. In each strip the slots with nodes come first, the rest are padding with every node -1.
All inputs are finite; a program needn't handle non-finite values. No bound on the sum of `land_mask` on one device may be relied on, other than what follows from the above.
Results may differ from a plain program's by a relative error of at most 0.00002.
Values sent between devices are 32-bit elements; how exact they have to be, the bound alone decides.
A program may use at most 64 MiB of HBM per device.

v0:
```python
import jax
import jax.numpy as jnp
from jax import lax
from jax.sharding import PartitionSpec as P

ITERS = 2
SWEEPS = 3
LATERAL = 1.0
VERTICAL = 2.0
GRAVITY = 1.0
NEIGHBOURS = (
    (0, -1, VERTICAL),
    (0, 1, VERTICAL),
    (1, -1, LATERAL),
    (1, 1, LATERAL),
    (2, -1, LATERAL),
    (2, 1, LATERAL),
)


def with_halo(block, sides, width):
    for axis, dim in sides:
        count = lax.axis_size(axis)
        forward = [(i, i + 1) for i in range(count - 1)]
        backward = [(target, source) for source, target in forward]
        low = lax.ppermute(
            lax.slice_in_dim(block, block.shape[dim] - width, None, axis=dim), axis, forward
        )
        high = lax.ppermute(lax.slice_in_dim(block, 0, width, axis=dim), axis, backward)
        block = jnp.concatenate([low, block, high], axis=dim)
    return block


def from_root(value, axis, source):
    kept = jnp.where(lax.axis_index(axis) == source, value, 0).astype(value.dtype)
    return lax.psum(kept, axis)


def beside(padded, axis_id, step):
    spans = [slice(1, -1), slice(1, -1), slice(1, -1)]
    spans[axis_id] = slice(1 + step, padded.shape[axis_id] - 1 + step)
    return padded[tuple(spans)]


def neighbor_weights(cond_pad, open_pad):
    centre = cond_pad[1:-1, 1:-1, 1:-1]
    centre_open = open_pad[1:-1, 1:-1, 1:-1]
    result = []
    for axis_id, step, factor in NEIGHBOURS:
        far = beside(cond_pad, axis_id, step)
        far_open = beside(open_pad, axis_id, step)
        result.append(factor * 2.0 * centre_open * far_open / (centre + far))
    return result


def relax(head_pad, weights, store, head_old, riv_diag, riv_rhs):
    total = store * head_old
    diagonal_sum = store
    for weight, (axis_id, step, factor) in zip(weights, NEIGHBOURS):
        total = total + weight * beside(head_pad, axis_id, step)
        diagonal_sum = diagonal_sum + weight
    total = total + GRAVITY * (weights[0] - weights[1]) + riv_rhs
    return total / (diagonal_sum + riv_diag)


def lookup(values_table, classes):
    result = jnp.zeros(classes.shape, jnp.float32)
    for class_id in range(values_table.shape[0]):
        result = jnp.where(classes == class_id, values_table[class_id], result)
    return result


def pad_dims(field, chosen_dims):
    widths = [(1, 1) if place in chosen_dims else (0, 0) for place in range(field.ndim)]
    return jnp.pad(field, widths)


def pick_heads(top_head, cells):
    breadth = top_head.shape[1]
    slots, width = cells.shape
    group = 16
    grouped = cells.reshape(slots // group, group * width)
    columns = jnp.arange(breadth, dtype=jnp.int32)[None, :]

    def one_group(flat_cells):
        picked_rows = jnp.take(top_head, flat_cells // breadth, axis=0)
        hit = columns == (flat_cells % breadth)[:, None]
        return jnp.sum(jnp.where(hit, picked_rows, 0.0), axis=1)

    return lax.map(one_group, grouped).reshape(slots, width)


def on_device(
    head_start,
    soil_class,
    land_mask,
    ks_table,
    alpha_table,
    store_table,
    section,
    cross_owner,
    cross_local,
    node_cell,
    bed_cond,
):
    layers, across, breadth = head_start.shape
    reach_rows = section.shape[0]
    node_count = section.shape[1]
    tile_count = lax.axis_size("tile")
    quarter = node_count // lax.axis_size("layer")
    node_first = lax.axis_index("layer") * quarter
    ks = lookup(ks_table, soil_class)
    alpha = lookup(alpha_table, soil_class)
    store = lookup(store_table, soil_class)
    landf = land_mask.astype(jnp.float32)[None]
    owners = cross_owner[0]
    positions = cross_local[0]
    node_cells = node_cell[0]
    bed_given = bed_cond[0]
    whole_section = lax.all_gather(section, "tile", axis=0, tiled=True)
    slot_section = jnp.take(whole_section, owners * reach_rows + positions, axis=0)
    in_tile = node_cells >= 0
    flat_index = jnp.where(in_tile, node_cells, across * breadth)
    bed_terms = jnp.where(in_tile, bed_given, 0.0)
    diag_top = (
        jnp.zeros((across * breadth,), jnp.float32)
        .at[flat_index.reshape(-1)]
        .add(bed_terms.reshape(-1), mode="drop")
    )
    rhs_top = (
        jnp.zeros((across * breadth,), jnp.float32)
        .at[flat_index.reshape(-1)]
        .add((bed_terms * slot_section).reshape(-1), mode="drop")
    )
    top_diag = diag_top.reshape(across, breadth)
    top_rhs = rhs_top.reshape(across, breadth)
    head_old, ks_here, alpha_here, store_here, land_here = (head_start, ks, alpha, store, landf)
    on_top = (lax.axis_index("layer") == 0).astype(jnp.float32)
    riv_diag = jnp.zeros((layers, across, breadth), jnp.float32).at[0].set(top_diag * on_top)
    riv_rhs = jnp.zeros((layers, across, breadth), jnp.float32).at[0].set(top_rhs * on_top)

    def head_halo(field):
        return pad_dims(with_halo(field, (("tile", 1), ("layer", 0)), 1), (2,))

    head = head_old
    for picard in range(ITERS):
        head_pad = head_halo(head)
        conduct = ks_here * jnp.exp(alpha_here * jnp.minimum(head, 0.0))
        both_pad = pad_dims(
            with_halo(jnp.stack([conduct, conduct * land_here]), (("tile", 2), ("layer", 1)), 1),
            (3,),
        )
        cond_pad = both_pad[0]
        open_pad = both_pad[1]
        weights = neighbor_weights(cond_pad, open_pad)
        for sweep in range(SWEEPS):
            if sweep > 0:
                head_pad = head_halo(head)
            head = relax(head_pad, weights, store_here, head_old, riv_diag, riv_rhs)
    top_head = from_root(head[0], "layer", 0)
    my_cells = lax.dynamic_slice_in_dim(node_cells, node_first, quarter, 1)
    my_bed = lax.dynamic_slice_in_dim(bed_given, node_first, quarter, 1)
    my_section = lax.dynamic_slice_in_dim(slot_section, node_first, quarter, 1)
    my_inside = my_cells >= 0
    node_head = pick_heads(top_head, jnp.where(my_inside, my_cells, 0))
    slot_in = jnp.where(my_inside, my_bed * (node_head - my_section), 0.0)
    dense = (
        jnp.zeros((reach_rows * tile_count, quarter), jnp.float32)
        .at[owners * reach_rows + positions]
        .add(slot_in)
    )
    inflow = lax.psum_scatter(dense, "tile", scatter_dimension=0, tiled=True)
    return (head, inflow)


def solution(mesh):
    placed = (
        P("layer", "tile", None),
        P("layer", "tile", None),
        P("tile", None),
        P(),
        P(),
        P(),
        P("tile", None),
        P("tile", None),
        P("tile", None),
        P("tile", None, None),
        P("tile", None, None),
    )
    return jax.shard_map(
        on_device,
        mesh=mesh,
        in_specs=placed,
        out_specs=(P("layer", "tile", None), P("tile", "layer")),
        check_vma=False,
    )
```

profile of v0, /device:TPU:8, one launch (start us, length us, event | category | flops | bytes accessed | tf_op | source)
XLA Modules:
  0.0 1032.4 jit_solution(11896485293692213495)
XLA Ops:
  7.2 1.8 fusion.137
  9.0 1.8 fusion.136
  11.7 17.8 %fusion.107 = (f32[1,2,64,512]{3,2,1,0:T(8,128)S(1)}, f32[2,64,512]{2,1,0:T(8,128)S(1)}, f32[2,64,512]{2,1,0:T(8,128)S(1)}, pred[2,64,512]{2,1,0:T(8,128)(4,1)S(...) fusion(f32[2,64,512]{2,1,0:T(8,128)} %param.17, ...), kind=kLoop, calls=%fused_computation.316 | loop fusion | flops 2555904 | bytes 2097248 | tf_op jit(solution)/shard_map/stack | solution.py:150
  31.0 3.0 collective-permute-start
  35.3 3.6 collective-permute-start.4
  40.6 7.1 collective-permute-start.7
  47.7 1.9 collective-permute-start.6
  49.8 3.9 collective-permute-start.3
  53.7 1.9 collective-permute-start.2
  56.7 4.8 collective-permute-done.3
  61.5 3.4 collective-permute-done.2
  66.5 8.5 add_add_fusion.1
  76.1 104.6 %all-gather.2.cloned.1.call-done = f32[2048,128]{1,0:T(8,128)} async-done(((f32[16,128]{1,0:T(8,128)}), f32[2048,128]{1,0:T(8,128)}) %all-gather.2.cloned.1.call-update) | async-done | bytes 1048592 | tf_op jit(solution)/shard_map/all_gather | solution.py:120
  180.6 1.9 gather_fusion.1
  182.6 1.7 bitcast_multiply_fusion.1
  184.3 171.3 %scatter_custom_fusion.1 = f32[32768]{0:T(1024)S(1)} fusion(s32[32768]{0:T(1024)} %bitcast.101, f32[32768]{0:T(1024)S(1)} %get-tuple-element.136, f32[]{:T(128)} %constant.189.clone.1), kind=kCustom, calls=%fused_computation.302 | custom fusion | flops 32768 | bytes 131584 | tf_op jit(solution)/shard_map/scatter-add | solution.py:128
  357.3 171.2 %scatter_custom_fusion = f32[32768]{0:T(1024)S(1)} fusion(s32[32768]{0:T(1024)} %bitcast.102, f32[32768]{0:T(1024)} %get-tuple-element.134, f32[]{:T(128)} %constant.189.clone.1), kind=kCustom, calls=%fused_computation.304 | custom fusion | flops 32768 | bytes 131584 | tf_op jit(solution)/shard_map/scatter-add | solution.py:133
  530.0 1.6 fusion.92
  534.0 3.0 collective-permute-start.8
  537.9 2.4 collective-permute-start.11
  540.3 3.4 collective-permute-start.10
  543.7 2.4 collective-permute-done.11
  546.1 2.7 collective-permute-done.10
  550.9 3.0 collective-permute-start.12
  554.8 1.9 collective-permute-start.15
  556.7 3.9 collective-permute-start.14
  560.6 2.0 collective-permute-done.15
  562.7 1.9 collective-permute-done.14
  567.5 3.1 collective-permute-start.20
  572.0 5.1 collective-permute-start.16
  578.0 1.9 collective-permute-start.19
  580.0 3.9 collective-permute-start.18
  583.9 1.9 collective-permute-start.23
  585.9 4.1 collective-permute-start.22
  590.0 2.6 collective-permute-done.23
  592.6 1.9 collective-permute-done.22
  598.7 3.0 collective-permute-start.24
  602.6 1.9 collective-permute-start.27
  604.6 3.9 collective-permute-start.26
  609.7 1.9 collective-permute-done.26
  613.7 4.8 collective-permute-start.28
  620.0 1.9 collective-permute-start.31
  621.9 3.9 collective-permute-start.30
  627.2 1.7 collective-permute-done.30
  630.5 75.9 %all-reduce.10.cloned.1.call-done = f32[64,512]{1,0:T(8,128)} async-done(((f32[64,512]{1,0:T(8,128)}), f32[64,512]{1,0:T(8,128)}) %all-reduce.10.cloned.1.call-update) | async-done | bytes 131088 | tf_op jit(solution)/shard_map/psum | solution.py:36
  706.4 54.5 %while.15 = (s32[]{:T(128)}, f32[16,512]{1,0:T(8,128)S(1)}, s32[16,512]{1,0:T(8,128)S(1)}, f32[64,512]{1,0:T(8,128)}, s32[]{:T(128)}, /*index=5*/s32[]{:T(128)}) while((s32[]{:T(128)}, f32[16,512]{1,0:T(8,128)S(1)}, s32[16,512]{1,0:T(8,128)S(1)}, f32[64,512]{1,0:T(8,128)}, s32[]{:T(128)}, /*index=5*/s32[]{:T(128)}) %tuple.130), condition=%wide.region_5.6_spmd.clone, body=%wide.region_3.5_spmd.clone.sunk | while | flops 1074690 | bytes 3175509 | solution.py:90
  706.4 3.0 gather_fusion
  709.9 2.9 gather_fusion
  713.3 2.9 gather_fusion
  716.7 2.9 gather_fusion
  720.1 2.9 gather_fusion
  723.5 2.9 gather_fusion
  726.9 2.9 gather_fusion
  730.3 2.9 gather_fusion
  733.7 2.9 gather_fusion
  737.1 2.9 gather_fusion
  740.5 2.9 gather_fusion
  743.9 2.9 gather_fusion
  747.3 2.9 gather_fusion
  750.7 2.9 gather_fusion
  754.1 2.9 gather_fusion
  757.5 2.9 gather_fusion
  761.0 2.6 scatter_custom_fusion.2
  763.6 262.3 %reduce-scatter.2.cloned.1.call-done = f32[16,32]{1,0:T(8,128)} async-done(((f32[2048,32]{1,0:T(8,128)}), f32[16,32]{1,0:T(8,128)}) %reduce-scatter.2.cloned.1.call-update) | async-done | bytes 2064 | tf_op jit(solution)/shard_map/reduce_scatter | solution.py:172
  (251 shorter events, 42.5 us)
Async XLA Ops:
  7.2 22.4 %copy-start = (f32[2,64,512]{2,1,0:T(8,128)S(1)}, f32[2,64,512]{2,1,0:T(8,128)}, u32[]{:S(2)}) copy-start(f32[2,64,512]{2,1,0:T(8,128)} %param.17) | copy-start | bytes 786436
  7.2 173.5 %all-gather.2.cloned.1.call-start = ((), (), s32[]{:S(2)}) async-start(), calls=%async_computation.1 | async-start | bytes 1056768 | tf_op jit(solution)/shard_map/all_gather | solution.py:120
  11.7 17.9 %copy-start.2 = (f32[64,512]{1,0:T(8,128)}, f32[64,512]{1,0:T(8,128)S(1)}, u32[]{:S(2)}) copy-start(f32[64,512]{1,0:T(8,128)S(1)} %convert_element_type.18) | copy-start | bytes 393220
  11.7 27.3 %copy-start.1 = (s32[1,256,128]{2,1,0:T(8,128)S(1)}, s32[1,256,128]{2,1,0:T(8,128)}, u32[]{:S(2)}) copy-start(s32[1,256,128]{2,1,0:T(8,128)} %param.26) | copy-start | bytes 393220
  29.6 10.4 %copy-start.22 = (s32[1,256]{1,0:T(1,128)S(1)}, s32[1,256]{1,0:T(1,128)}, u32[]{:S(2)}) copy-start(s32[1,256]{1,0:T(1,128)} %param.25) | copy-start | bytes 3076
  29.6 10.4 %copy-start.23 = (s32[1,256]{1,0:T(1,128)S(1)}, s32[1,256]{1,0:T(1,128)}, u32[]{:S(2)}) copy-start(s32[1,256]{1,0:T(1,128)} %param.24) | copy-start | bytes 3076
  29.7 19.9 %collective-permute-start.1 = (f32[2,2,1,512]{3,2,1,0:T(1,128)S(1)}, f32[2,2,1,512]{3,2,1,0:T(1,128)S(1)}, u32[]{:S(2)}, u32[]{:S(2)}) collective-permute-start(f32[2,2,1,512]{3,2,1,0:T(1,128)S(1)} %get-tuple-element.168), channel_id=1, source_target_pairs={{4,0},{8,4},{12,8},{16,12},{20,16},{24,20},{28,24},{32,28},{36,32}... | collective-permute-start | bytes 24584 | tf_op jit(solution)/shard_map/ppermute | solution.py:29
  31.0 18.6 %collective-permute-start = (f32[2,2,1,512]{3,2,1,0:T(1,128)S(1)}, f32[2,2,1,512]{3,2,1,0:T(1,128)S(1)}, u32[]{:S(2)}, u32[]{:S(2)}) collective-permute-start(f32[2,2,1,512]{3,2,1,0:T(1,128)S(1)} %get-tuple-element.167), channel_id=1, source_target_pairs={{0,4},{4,8},{8,12},{12,16},{16,20},{20,24},{24,28},{28,32},{32,36}... | collective-permute-start | bytes 24584 | tf_op jit(solution)/shard_map/ppermute | solution.py:26
  34.0 6.4 collective-permute-start.5
  35.3 5.1 collective-permute-start.4
  39.0 667.3 %all-reduce.10.cloned.1.call-start = ((), (), s32[]{:S(2)}) async-start(), calls=%async_computation.2 | async-start | bytes 262144 | tf_op jit(solution)/shard_map/psum | solution.py:36
  40.5 15.1 %copy-start.21 = (f32[12]{0:T(128)S(1)}, f32[12]{0:T(128)}, u32[]{:S(2)}) copy-start(f32[12]{0:T(128)} %param.22) | copy-start | bytes 148
  40.6 15.8 %collective-permute-start.7 = (f32[1,66,512]{2,1,0:T(8,128)S(1)}, f32[1,66,512]{2,1,0:T(8,128)S(1)}, u32[]{:S(2)}, u32[]{:S(2)}) collective-permute-start(f32[1,66,512]{2,1,0:T(8,128)S(1)} %get-tuple-element.180), channel_id=1, source_target_pairs={{1,0},{2,1},{3,2},{5,4},{6,5},{7,6},{9,8},{10,9},{11,10},{13,12},{... | collective-permute-start | bytes 405512 | tf_op jit(solution)/shard_map/ppermute | solution.py:29
  47.7 8.7 collective-permute-start.6
  49.8 11.8 %collective-permute-start.3 = (f32[2,1,66,512]{3,2,1,0:T(8,128)S(1)}, f32[2,1,66,512]{3,2,1,0:T(8,128)S(1)}, u32[]{:S(2)}, u32[]{:S(2)}) collective-permute-start(f32[2,1,66,512]{3,2,1,0:T(8,128)S(1)} %get-tuple-element.164), channel_id=1, source_target_pairs={{1,0},{2,1},{3,2},{5,4},{6,5},{7,6},{9,8},{10,9},{11,10},{13,12},{... | collective-permute-start | bytes 811016 | tf_op jit(solution)/shard_map/ppermute | solution.py:29
  53.7 11.2 %collective-permute-start.2 = (f32[2,1,66,512]{3,2,1,0:T(8,128)S(1)}, f32[2,1,66,512]{3,2,1,0:T(8,128)S(1)}, u32[]{:S(2)}, u32[]{:S(2)}) collective-permute-start(f32[2,1,66,512]{3,2,1,0:T(8,128)S(1)} %get-tuple-element.163), channel_id=1, source_target_pairs={{0,1},{1,2},{2,3},{4,5},{5,6},{6,7},{8,9},{9,10},{10,11},{12,13},{... | collective-permute-start | bytes 811016 | tf_op jit(solution)/shard_map/ppermute | solution.py:26
  56.4 9.1 copy-start.6
  56.4 9.0 copy-start.8
  65.5 0.8 copy-start.13
  65.5 0.9 copy-start.14
  65.5 0.9 copy-start.15
  65.5 0.9 copy-start.16
  65.5 0.9 copy-start.17
  65.5 1.0 copy-start.18
  65.5 1.0 copy-start.19
  65.5 1.0 copy-start.20
  66.5 8.5 copy-start.7
  66.5 8.5 copy-start.9
  357.3 180.6 %copy-start.4 = (f32[1,64,512]{2,1,0:T(8,128)}, f32[1,64,512]{2,1,0:T(8,128)S(1)}, u32[]{:S(2)}) copy-start(f32[1,64,512]{2,1,0:T(8,128)S(1)} %mul.274) | copy-start | bytes 393220
  532.7 4.3 collective-permute-start.9
  534.0 3.8 collective-permute-start.8
  537.9 8.2 collective-permute-start.11
  540.3 8.4 collective-permute-start.10
  549.5 4.3 collective-permute-start.13
  550.9 3.8 collective-permute-start.12
  554.8 7.9 collective-permute-start.15
  556.7 7.9 collective-permute-start.14
  565.2 0.9 copy-start.3
  566.2 10.9 %collective-permute-start.21 = (f32[2,1,512]{2,1,0:T(1,128)S(1)}, f32[2,1,512]{2,1,0:T(1,128)S(1)}, u32[]{:S(2)}, u32[]{:S(2)}) collective-permute-start(f32[2,1,512]{2,1,0:T(1,128)S(1)} %get-tuple-element.186), channel_id=1, source_target_pairs={{4,0},{8,4},{12,8},{16,12},{20,16},{24,20},{28,24},{32,28},{36,32}... | collective-permute-start | bytes 12296 | tf_op jit(solution)/shard_map/ppermute | solution.py:29
  567.5 9.6 collective-permute-start.20
  570.7 6.5 collective-permute-start.17
  572.0 6.0 collective-permute-start.16
  578.0 16.8 %collective-permute-start.19 = (f32[2,1,66,512]{3,2,1,0:T(8,128)S(1)}, f32[2,1,66,512]{3,2,1,0:T(8,128)S(1)}, u32[]{:S(2)}, u32[]{:S(2)}) collective-permute-start(f32[2,1,66,512]{3,2,1,0:T(8,128)S(1)} %get-tuple-element.162), channel_id=1, source_target_pairs={{1,0},{2,1},{3,2},{5,4},{6,5},{7,6},{9,8},{10,9},{11,10},{13,12},{... | collective-permute-start | bytes 811016 | tf_op jit(solution)/shard_map/ppermute | solution.py:29
  580.0 14.9 %collective-permute-start.18 = (f32[2,1,66,512]{3,2,1,0:T(8,128)S(1)}, f32[2,1,66,512]{3,2,1,0:T(8,128)S(1)}, u32[]{:S(2)}, u32[]{:S(2)}) collective-permute-start(f32[2,1,66,512]{3,2,1,0:T(8,128)S(1)} %get-tuple-element.161), channel_id=1, source_target_pairs={{0,1},{1,2},{2,3},{4,5},{5,6},{6,7},{8,9},{9,10},{10,11},{12,13},{... | collective-permute-start | bytes 811016 | tf_op jit(solution)/shard_map/ppermute | solution.py:26
  583.9 8.7 collective-permute-start.23
  585.9 8.7 collective-permute-start.22
  596.4 0.9 copy-start.5
  597.4 4.3 collective-permute-start.25
  598.7 3.8 collective-permute-start.24
  602.6 7.0 collective-permute-start.27
  604.6 7.0 collective-permute-start.26
  612.4 6.1 collective-permute-start.29
  613.7 5.6 collective-permute-start.28
  620.0 7.2 collective-permute-start.31
  621.9 7.0 collective-permute-start.30
  629.7 76.7 %copy-start.10 = (f32[2,64,512]{2,1,0:T(8,128)}, f32[2,64,512]{2,1,0:T(8,128)S(1)}, u32[]{:S(2)}) copy-start(f32[2,64,512]{2,1,0:T(8,128)S(1)} %div.91) | copy-start | bytes 786436
  630.4 395.5 %reduce-scatter.2.cloned.1.call-start = ((), (), s32[]{:S(2)}) async-start(), calls=%async_computation.3 | async-start | bytes 1056768 | tf_op jit(solution)/shard_map/reduce_scatter | solution.py:172
  706.4 54.6 %copy-start.11 = (f32[1,256,128]{2,1,0:T(8,128)S(1)}, f32[1,256,128]{2,1,0:T(8,128)}, u32[]{:S(2)}) copy-start(f32[1,256,128]{2,1,0:T(8,128)} %param.27) | copy-start | bytes 393220
  706.4 54.6 %copy-start.12 = (f32[256,128]{1,0:T(8,128)S(1)}, f32[256,128]{1,0:T(8,128)}, u32[]{:S(2)}) copy-start(f32[256,128]{1,0:T(8,128)} %get-tuple-element.135) | copy-start | bytes 393220
Sparse Core Ops, SparseCore 0:
  39.1 141.4 all-gather.1
  630.6 75.7 all-reduce.9
  763.7 262.1 reduce-scatter.1
where the time goes:
time: 1030 us
  waiting for transfers between devices  475 us (46%)
  other arithmetic  393 us (38%)
  starting transfers between devices  89.4 us (9%)
  local copies, waits for them, and re-layouts  59.6 us (6%)
  between operations  14.7 us (1%)
    reduce_scatter x1, waiting for transfers between devices, on_device(): inflow = lax.psum_scatter(dense, 'tile', scatter_dimension=0, tiled=True)  262 us
    scatter-add x1, other arithmetic, on_device(): diag_top = jnp.zeros((across * breadth,), jnp.float32).at[flat_index.resh...  171 us
    scatter-add x1, other arithmetic, on_device(): rhs_top = jnp.zeros((across * breadth,), jnp.float32).at[flat_index.resha...  171 us
    all_gather x1, waiting for transfers between devices, on_device(): whole_section = lax.all_gather(section, 'tile', axis=0, tiled=True)  105 us
    psum x1, waiting for transfers between devices, from_root(): return lax.psum(kept, axis)  75.9 us
    ppermute x16, starting transfers between devices, with_halo(): lax.ppermute(lax.slice_in_dim(block, block.shape[dim] - width, None, axis...  55.8 us
    gather x16, local copies, waits for them, and re-layouts, one_group(): picked_rows = jnp.take(top_head, flat_cells // breadth, axis=0)  47 us
    ppermute x16, starting transfers between devices, with_halo(): lax.ppermute(lax.slice_in_dim(block, 0, width, axis=dim), axis, backward)  33.4 us
  transfers between devices with their start and end apart: 35, of which 20 were waited for; matrix products, arithmetic and copies ran while one was open for 1% of the time, Pallas kernels for 0%

commit v1 on v0

--- a/solution.py
+++ b/solution.py
@@ -33,7 +33,7 @@
 
 def from_root(value, axis, source):
     kept = jnp.where(lax.axis_index(axis) == source, value, 0).astype(value.dtype)
-    return lax.psum(kept, axis)
+    return jnp.sum(lax.all_gather(kept, axis), axis=0)
 
 
 def beside(padded, axis_id, step):

time: 1030 us -> 969 us (0.941)
  waiting for transfers between devices: 475 us -> 417 us
  local copies, waits for them, and re-layouts: 59.6 us -> 38.6 us
  blocking collectives: 0 us -> 13.9 us
    psum x1 -> x0, waiting for transfers between devices: 75.9 us -> none  [from_root(): return lax.psum(kept, axis)]
    gather x16, local copies, waits for them, and re-layouts: 47 us -> 25.9 us  [one_group(): picked_rows = jnp.take(top_head, flat_cells // breadth, axis=0)]
    reduce_scatter x1, waiting for transfers between devices: 262 us -> 281 us  [on_device(): inflow = lax.psum_scatter(dense, 'tile', scatter_dimension=0, tiled=True)]
    all_gather x0 -> x1, blocking collectives: none -> 13.9 us  [from_root(): return jnp.sum(lax.all_gather(kept, axis), axis=0)]
  transfers between devices with their start and end apart: 35 -> 34, of which waited for: 20 -> 19; matrix products, arithmetic and copies ran while one was open for 1% -> 1% of each run, Pallas kernels for 0% -> 0%
where the time goes in v1:
time: 969 us; the launch traced here: 967 us
  waiting for transfers between devices  417 us (43%)
  other arithmetic  392 us (40%)
  starting transfers between devices  89.3 us (9%)
  local copies, waits for them, and re-layouts  38.6 us (4%)
  between operations  15.1 us (2%)
  blocking collectives  13.9 us (1%)
    reduce_scatter x1, waiting for transfers between devices, on_device(): inflow = lax.psum_scatter(dense, 'tile', scatter_dimension=0, tiled=True)  281 us
    scatter-add x1, other arithmetic, on_device(): diag_top = jnp.zeros((across * breadth,), jnp.float32).at[flat_index.resh...  171 us
    scatter-add x1, other arithmetic, on_device(): rhs_top = jnp.zeros((across * breadth,), jnp.float32).at[flat_index.resha...  171 us
    all_gather x1, waiting for transfers between devices, on_device(): whole_section = lax.all_gather(section, 'tile', axis=0, tiled=True)  105 us
    ppermute x16, starting transfers between devices, with_halo(): lax.ppermute(lax.slice_in_dim(block, block.shape[dim] - width, None, axis...  55.8 us
    ppermute x16, starting transfers between devices, with_halo(): lax.ppermute(lax.slice_in_dim(block, 0, width, axis=dim), axis, backward)  33.4 us
    gather x16, local copies, waits for them, and re-layouts, one_group(): picked_rows = jnp.take(top_head, flat_cells // breadth, axis=0)  25.9 us
  transfers between devices with their start and end apart: 34, of which 19 were waited for; matrix products, arithmetic and copies ran while one was open for 1% of the time, Pallas kernels for 0%

profile of v1, /device:TPU:8, one launch (start us, length us, event | category | flops | bytes accessed | tf_op | source)
XLA Modules:
  0.0 967.5 jit_solution(8029153332786504947)
XLA Ops:
  7.2 1.8 fusion.136
  9.0 1.8 fusion.135
  11.8 17.8 %fusion.106 = (f32[1,2,64,512]{3,2,1,0:T(8,128)S(1)}, f32[2,64,512]{2,1,0:T(8,128)S(1)}, f32[2,64,512]{2,1,0:T(8,128)S(1)}, pred[2,64,512]{2,1,0:T(8,128)(4,1)S(...) fusion(f32[2,64,512]{2,1,0:T(8,128)} %param.17, ...), kind=kLoop, calls=%fused_computation.315 | loop fusion | flops 2555904 | bytes 2097248 | tf_op jit(solution)/shard_map/stack | solution.py:150
  30.9 3.0 collective-permute-start
  35.3 3.6 collective-permute-start.4
  40.6 7.1 collective-permute-start.7
  47.7 1.9 collective-permute-start.6
  49.8 3.9 collective-permute-start.3
  53.7 1.9 collective-permute-start.2
  56.7 4.8 collective-permute-done.3
  61.6 3.4 collective-permute-done.2
  66.6 8.3 add_add_fusion.1
  76.0 104.6 %all-gather.2.cloned.1.call-done = f32[2048,128]{1,0:T(8,128)} async-done(((f32[16,128]{1,0:T(8,128)}), f32[2048,128]{1,0:T(8,128)}) %all-gather.2.cloned.1.call-update) | async-done | bytes 1048592 | tf_op jit(solution)/shard_map/all_gather | solution.py:120
  180.6 1.9 gather_fusion.1
  182.6 1.7 bitcast_multiply_fusion.1
  184.3 171.3 %scatter_custom_fusion.1 = f32[32768]{0:T(1024)S(1)} fusion(s32[32768]{0:T(1024)} %bitcast.99, f32[32768]{0:T(1024)S(1)} %get-tuple-element.136, f32[]{:T(128)} %constant.189.clone.1), kind=kCustom, calls=%fused_computation.301 | custom fusion | flops 32768 | bytes 131584 | tf_op jit(solution)/shard_map/scatter-add | solution.py:128
  357.2 171.2 %scatter_custom_fusion = f32[32768]{0:T(1024)S(1)} fusion(s32[32768]{0:T(1024)} %bitcast.100, f32[32768]{0:T(1024)} %get-tuple-element.134, f32[]{:T(128)} %constant.189.clone.1), kind=kCustom, calls=%fused_computation.303 | custom fusion | flops 32768 | bytes 131584 | tf_op jit(solution)/shard_map/scatter-add | solution.py:133
  530.0 1.6 fusion.91
  533.9 3.0 collective-permute-start.8
  537.8 2.4 collective-permute-start.11
  540.3 3.4 collective-permute-start.10
  543.7 2.4 collective-permute-done.11
  546.1 2.7 collective-permute-done.10
  550.8 3.0 collective-permute-start.12
  554.7 1.9 collective-permute-start.15
  556.7 3.9 collective-permute-start.14
  560.6 2.0 collective-permute-done.15
  562.6 1.9 collective-permute-done.14
  567.5 3.1 collective-permute-start.20
  571.9 5.1 collective-permute-start.16
  578.0 1.9 collective-permute-start.19
  579.9 3.9 collective-permute-start.18
  583.9 1.9 collective-permute-start.23
  585.8 4.1 collective-permute-start.22
  590.0 2.6 collective-permute-done.23
  592.6 1.9 collective-permute-done.22
  598.7 3.0 collective-permute-start.24
  603.2 1.9 collective-permute-start.27
  605.2 3.9 collective-permute-start.26
  610.5 1.7 collective-permute-done.26
  614.3 4.8 collective-permute-start.28
  619.9 1.9 collective-permute-start.31
  621.9 3.9 collective-permute-start.30
  627.0 1.9 collective-permute-done.30
  629.7 13.9 %all_gather.8 = f32[4,64,512]{2,1,0:T(8,128)S(1)} all-gather(f32[1,64,512]{2,1,0:T(8,128)S(1)} %slice_select_fusion), channel_id=1, replica_groups=mesh['tile'=128,'layer'=4] {'layer'}, dimensions={0}, use_global_device_ids=true | all-gather | bytes 655360 | tf_op jit(solution)/shard_map/all_gather | solution.py:36
  643.7 33.5 %while.15 = (s32[]{:T(128)}, f32[16,512]{1,0:T(8,128)S(1)}, s32[16,512]{1,0:T(8,128)S(1)}, f32[64,512]{1,0:T(8,128)S(1)}, s32[]{:T(128)}, /*index=5*/s32[]{:T(128)}) while((s32[]{:T(128)}, f32[16,512]{1,0:T(8,128)S(1)}, s32[16,512]{1,0:T(8,128)S(1)}, f32[64,512]{1,0:T(8,128)S(1)}, s32[]{:T(128)}, /*index=5*/s32[]{:T(128)}) %tuple.130), condition=%wide.region_5.6_spmd.clone, body=%wide.region_3.5_spmd.clone.sunk | while | flops 1074690 | bytes 3175509 | solution.py:90
  643.7 1.6 gather_fusion
  645.8 1.6 gather_fusion
  647.9 1.6 gather_fusion
  650.0 1.6 gather_fusion
  652.1 1.6 gather_fusion
  654.2 1.6 gather_fusion
  656.3 1.6 gather_fusion
  658.4 1.6 gather_fusion
  660.5 1.6 gather_fusion
  662.6 1.6 gather_fusion
  664.7 1.6 gather_fusion
  666.8 1.6 gather_fusion
  668.9 1.6 gather_fusion
  671.0 1.6 gather_fusion
  673.0 1.6 gather_fusion
  675.1 1.6 gather_fusion
  677.3 2.6 scatter_custom_fusion.2
  679.9 280.7 %reduce-scatter.2.cloned.1.call-done = f32[16,32]{1,0:T(8,128)} async-done(((f32[2048,32]{1,0:T(8,128)}), f32[16,32]{1,0:T(8,128)}) %reduce-scatter.2.cloned.1.call-update) | async-done | bytes 2064 | tf_op jit(solution)/shard_map/reduce_scatter | solution.py:172
  (250 shorter events, 41.8 us)
Async XLA Ops:
  7.2 22.4 %copy-start = (f32[2,64,512]{2,1,0:T(8,128)S(1)}, f32[2,64,512]{2,1,0:T(8,128)}, u32[]{:S(2)}) copy-start(f32[2,64,512]{2,1,0:T(8,128)} %param.17) | copy-start | bytes 786436
  7.2 173.4 %all-gather.2.cloned.1.call-start = ((), (), s32[]{:S(2)}) async-start(), calls=%async_computation.1 | async-start | bytes 1056768 | tf_op jit(solution)/shard_map/all_gather | solution.py:120
  11.7 17.9 %copy-start.2 = (f32[64,512]{1,0:T(8,128)}, f32[64,512]{1,0:T(8,128)S(1)}, u32[]{:S(2)}) copy-start(f32[64,512]{1,0:T(8,128)S(1)} %convert_element_type.18) | copy-start | bytes 393220
  11.7 27.3 %copy-start.1 = (s32[1,256,128]{2,1,0:T(8,128)S(1)}, s32[1,256,128]{2,1,0:T(8,128)}, u32[]{:S(2)}) copy-start(s32[1,256,128]{2,1,0:T(8,128)} %param.26) | copy-start | bytes 393220
  29.5 10.4 %copy-start.22 = (s32[1,256]{1,0:T(1,128)S(1)}, s32[1,256]{1,0:T(1,128)}, u32[]{:S(2)}) copy-start(s32[1,256]{1,0:T(1,128)} %param.25) | copy-start | bytes 3076
  29.5 10.4 %copy-start.23 = (s32[1,256]{1,0:T(1,128)S(1)}, s32[1,256]{1,0:T(1,128)}, u32[]{:S(2)}) copy-start(s32[1,256]{1,0:T(1,128)} %param.24) | copy-start | bytes 3076
  29.6 20.0 %collective-permute-start.1 = (f32[2,2,1,512]{3,2,1,0:T(1,128)S(1)}, f32[2,2,1,512]{3,2,1,0:T(1,128)S(1)}, u32[]{:S(2)}, u32[]{:S(2)}) collective-permute-start(f32[2,2,1,512]{3,2,1,0:T(1,128)S(1)} %get-tuple-element.168), channel_id=1, source_target_pairs={{4,0},{8,4},{12,8},{16,12},{20,16},{24,20},{28,24},{32,28},{36,32}... | collective-permute-start | bytes 24584 | tf_op jit(solution)/shard_map/ppermute | solution.py:29
  30.9 18.7 %collective-permute-start = (f32[2,2,1,512]{3,2,1,0:T(1,128)S(1)}, f32[2,2,1,512]{3,2,1,0:T(1,128)S(1)}, u32[]{:S(2)}, u32[]{:S(2)}) collective-permute-start(f32[2,2,1,512]{3,2,1,0:T(1,128)S(1)} %get-tuple-element.167), channel_id=1, source_target_pairs={{0,4},{4,8},{8,12},{12,16},{16,20},{20,24},{24,28},{28,32},{32,36}... | collective-permute-start | bytes 24584 | tf_op jit(solution)/shard_map/ppermute | solution.py:26
  34.0 6.5 collective-permute-start.5
  35.3 5.2 collective-permute-start.4
  39.0 921.7 %reduce-scatter.2.cloned.1.call-start = ((), (), s32[]{:S(2)}) async-start(), calls=%async_computation.2 | async-start | bytes 1056768 | tf_op jit(solution)/shard_map/reduce_scatter | solution.py:172
  40.5 15.1 %copy-start.21 = (f32[12]{0:T(128)S(1)}, f32[12]{0:T(128)}, u32[]{:S(2)}) copy-start(f32[12]{0:T(128)} %param.22) | copy-start | bytes 148
  40.6 15.8 %collective-permute-start.7 = (f32[1,66,512]{2,1,0:T(8,128)S(1)}, f32[1,66,512]{2,1,0:T(8,128)S(1)}, u32[]{:S(2)}, u32[]{:S(2)}) collective-permute-start(f32[1,66,512]{2,1,0:T(8,128)S(1)} %get-tuple-element.180), channel_id=1, source_target_pairs={{1,0},{2,1},{3,2},{5,4},{6,5},{7,6},{9,8},{10,9},{11,10},{13,12},{... | collective-permute-start | bytes 405512 | tf_op jit(solution)/shard_map/ppermute | solution.py:29
  47.7 8.7 collective-permute-start.6
  49.8 11.8 %collective-permute-start.3 = (f32[2,1,66,512]{3,2,1,0:T(8,128)S(1)}, f32[2,1,66,512]{3,2,1,0:T(8,128)S(1)}, u32[]{:S(2)}, u32[]{:S(2)}) collective-permute-start(f32[2,1,66,512]{3,2,1,0:T(8,128)S(1)} %get-tuple-element.164), channel_id=1, source_target_pairs={{1,0},{2,1},{3,2},{5,4},{6,5},{7,6},{9,8},{10,9},{11,10},{13,12},{... | collective-permute-start | bytes 811016 | tf_op jit(solution)/shard_map/ppermute | solution.py:29
  53.7 11.2 %collective-permute-start.2 = (f32[2,1,66,512]{3,2,1,0:T(8,128)S(1)}, f32[2,1,66,512]{3,2,1,0:T(8,128)S(1)}, u32[]{:S(2)}, u32[]{:S(2)}) collective-permute-start(f32[2,1,66,512]{3,2,1,0:T(8,128)S(1)} %get-tuple-element.163), channel_id=1, source_target_pairs={{0,1},{1,2},{2,3},{4,5},{5,6},{6,7},{8,9},{9,10},{10,11},{12,13},{... | collective-permute-start | bytes 811016 | tf_op jit(solution)/shard_map/ppermute | solution.py:26
  56.4 9.1 copy-start.6
  56.4 9.1 copy-start.8
  65.5 0.8 copy-start.13
  65.5 0.9 copy-start.14
  65.5 0.9 copy-start.15
  65.5 0.9 copy-start.16
  65.5 0.9 copy-start.17
  65.5 1.0 copy-start.18
  65.5 1.0 copy-start.19
  65.5 1.0 copy-start.20
  66.5 8.4 copy-start.7
  66.6 8.4 copy-start.9
  357.2 180.6 %copy-start.4 = (f32[1,64,512]{2,1,0:T(8,128)}, f32[1,64,512]{2,1,0:T(8,128)S(1)}, u32[]{:S(2)}) copy-start(f32[1,64,512]{2,1,0:T(8,128)S(1)} %mul.274) | copy-start | bytes 393220
  532.6 4.3 collective-permute-start.9
  533.9 3.8 collective-permute-start.8
  537.8 8.2 collective-permute-start.11
  540.3 8.4 collective-permute-start.10
  549.5 4.3 collective-permute-start.13
  550.8 3.8 collective-permute-start.12
  554.7 7.9 collective-permute-start.15
  556.7 7.9 collective-permute-start.14
  565.2 0.9 copy-start.3
  566.2 10.9 %collective-permute-start.21 = (f32[2,1,512]{2,1,0:T(1,128)S(1)}, f32[2,1,512]{2,1,0:T(1,128)S(1)}, u32[]{:S(2)}, u32[]{:S(2)}) collective-permute-start(f32[2,1,512]{2,1,0:T(1,128)S(1)} %get-tuple-element.186), channel_id=1, source_target_pairs={{4,0},{8,4},{12,8},{16,12},{20,16},{24,20},{28,24},{32,28},{36,32}... | collective-permute-start | bytes 12296 | tf_op jit(solution)/shard_map/ppermute | solution.py:29
  567.5 9.6 collective-permute-start.20
  570.6 6.5 collective-permute-start.17
  571.9 6.0 collective-permute-start.16
  578.0 16.8 %collective-permute-start.19 = (f32[2,1,66,512]{3,2,1,0:T(8,128)S(1)}, f32[2,1,66,512]{3,2,1,0:T(8,128)S(1)}, u32[]{:S(2)}, u32[]{:S(2)}) collective-permute-start(f32[2,1,66,512]{3,2,1,0:T(8,128)S(1)} %get-tuple-element.162), channel_id=1, source_target_pairs={{1,0},{2,1},{3,2},{5,4},{6,5},{7,6},{9,8},{10,9},{11,10},{13,12},{... | collective-permute-start | bytes 811016 | tf_op jit(solution)/shard_map/ppermute | solution.py:29
  579.9 14.9 %collective-permute-start.18 = (f32[2,1,66,512]{3,2,1,0:T(8,128)S(1)}, f32[2,1,66,512]{3,2,1,0:T(8,128)S(1)}, u32[]{:S(2)}, u32[]{:S(2)}) collective-permute-start(f32[2,1,66,512]{3,2,1,0:T(8,128)S(1)} %get-tuple-element.161), channel_id=1, source_target_pairs={{0,1},{1,2},{2,3},{4,5},{5,6},{6,7},{8,9},{9,10},{10,11},{12,13},{... | collective-permute-start | bytes 811016 | tf_op jit(solution)/shard_map/ppermute | solution.py:26
  583.9 8.7 collective-permute-start.23
  585.8 8.7 collective-permute-start.22
  596.4 0.9 copy-start.5
  597.4 4.3 collective-permute-start.25
  598.7 3.8 collective-permute-start.24
  603.2 7.2 collective-permute-start.27
  605.2 7.0 collective-permute-start.26
  613.0 6.3 collective-permute-start.29
  614.3 5.6 collective-permute-start.28
  619.9 7.0 collective-permute-start.31
  621.9 7.0 collective-permute-start.30
  629.7 14.0 %copy-start.10 = (f32[2,64,512]{2,1,0:T(8,128)}, f32[2,64,512]{2,1,0:T(8,128)S(1)}, u32[]{:S(2)}) copy-start(f32[2,64,512]{2,1,0:T(8,128)S(1)} %div.91) | copy-start | bytes 786436
  643.6 33.6 %copy-start.11 = (f32[1,256,128]{2,1,0:T(8,128)S(1)}, f32[1,256,128]{2,1,0:T(8,128)}, u32[]{:S(2)}) copy-start(f32[1,256,128]{2,1,0:T(8,128)} %param.27) | copy-start | bytes 393220
  643.7 33.6 %copy-start.12 = (f32[256,128]{1,0:T(8,128)S(1)}, f32[256,128]{1,0:T(8,128)}, u32[]{:S(2)}) copy-start(f32[256,128]{1,0:T(8,128)} %get-tuple-element.135) | copy-start | bytes 393220
Sparse Core Ops, SparseCore 0:
  39.1 141.4 all-gather.1
  680.1 280.5 reduce-scatter.1
